TPU v7x, 32 devices: a whole 2x2x4 slice. The times are simulated.
32 devices in a mesh: vec: 4 (over z), row: 8 (over y, x, core).
Axes of the slice: x: 2, y: 2, z: 4, core: 2. Of those that a mesh axis runs over, the one named last changes fastest.
Arguments:
- chol_vectors: float32 [128, 1024, 1024], P('vec', 'row'), may hold values from -16 to 16, as said below
Outputs:
- rotated: float32 [128, 1024, 1024], P('vec', 'row')
- rotation: float32 [1024, 1024], P('row')
Inputs may be any that keep to these rules, and one draw needn't show every extreme that they name: Every matrix chol_vectors[P] is symmetric in its last two dimensions.
All inputs are finite; a program needn't handle non-finite values.
Results may differ from a plain program's by a relative error of at most 0.00014.
Values sent between devices are 32-bit elements; how exact they have to be, the bound alone decides.
No kernel may reach another device: no remote copies, remote signals or barrier semaphores. Data moves between devices by JAX's collectives and lax.ppermute only.
A program may use at most 128 MiB of HBM per device.

v0:
```python
import jax
import jax.numpy as jnp
from jax import lax
from jax.sharding import PartitionSpec as P

ITERS = 2
step_gain = 0.2


def shards(chol_vectors):
    row_count = chol_vectors.shape[1]
    orbitals = chol_vectors.shape[2]
    offset = lax.axis_index("row") * row_count
    highest = lax.Precision.HIGHEST
    local_rows = lax.broadcasted_iota(jnp.int32, (row_count, orbitals), 0) + offset
    local_cols = lax.broadcasted_iota(jnp.int32, (row_count, orbitals), 1)
    identity_rows = (local_rows == local_cols).astype(jnp.float32)
    current = chol_vectors
    rotation = identity_rows
    for iteration in range(ITERS):
        block = lax.dynamic_slice_in_dim(current, offset, row_count, 2)
        diagonal = jnp.diagonal(block, axis1=1, axis2=2)
        own_part = jnp.einsum("pjk,pj->jk", current, diagonal, precision=highest)
        diagonal_all = lax.all_gather(diagonal, "row", axis=1, tiled=True)
        other_part = jnp.einsum("pjk,pk->jk", current, diagonal_all, precision=highest)
        gradient = lax.psum(own_part - other_part, "vec")
        squares = lax.psum(jnp.sum(gradient * gradient), "row")
        norm = jnp.sqrt(squares / (orbitals * orbitals) + 1e-06)
        generator = step_gain / jnp.sqrt(jnp.float32(orbitals)) * gradient / norm
        generator_full = lax.all_gather(generator, "row", axis=0, tiled=True)
        identity_full = jnp.eye(orbitals, dtype=jnp.float32)
        step_full = (
            identity_full
            + generator_full
            + 0.5 * jnp.dot(generator_full, generator_full, precision=highest)
        )
        step_local = lax.dynamic_slice_in_dim(step_full, offset, row_count, 0)
        if iteration == 0:
            rotation = step_local
        else:
            rotation = jnp.dot(rotation, step_full, precision=highest)
        product_left = jnp.einsum("pjk,kl->pjl", current, step_full, precision=highest)
        columns = lax.all_to_all(product_left, "row", split_axis=2, concat_axis=1, tiled=True)
        current = jnp.einsum("pim,ik->pmk", columns, step_full, precision=highest)
    return (current, rotation)


def solution(mesh):
    placed = (P("vec", "row", None),)
    return jax.shard_map(
        shards,
        mesh=mesh,
        in_specs=placed,
        out_specs=(P("vec", "row", None), P("row", None)),
        check_vma=False,
    )
```

profile of v0, /device:TPU:0, one launch (start us, length us, event | category | flops | bytes accessed | tf_op | source)
XLA Modules:
  0.0 1111.6 jit_solution(9601472853553550261)
XLA Ops:
  7.2 1.7 constant_dynamic-slice_fusion.1
  9.0 4.7 copy.37
  13.6 1.9 gather_fusion
  15.5 11.3 %all_gather.12 = f32[32,1024]{0,1:T(8,128)S(1)} all-gather(f32[32,128]{0,1:T(8,128)S(1)} %bitcast.73), channel_id=1, replica_groups=mesh['vec'=4,'row'=8] {'row'}, dimensions={1}, use_global_device_ids=true | all-gather | bytes 147456 | tf_op jit(solution)/shard_map/all_gather | solution.py:24
  26.8 0.2 copy.38
  27.0 8.4 multiply_reduce_fusion.1
  35.4 22.4 %fusion.2 = f32[128,1,1024]{2,1,0:T(1,128)S(1)} fusion(f32[32,128,1]{0,2,1:T(1,128)S(1)} %bitcast.74, f32[32,128,1024]{2,1,0:T(8,128)} %param.1), kind=kOutput, calls=%fused_computation.6 | convolution fusion | flops 50331648 | bytes 17317888 | tf_op jit(solution)/shard_map/pjk,pj->jk/dot_general | solution.py:23
  57.7 0.9 bitcast_subtract_fusion.1
  58.7 0.0 all-gather.3.cloned.1.call-start
  58.7 38.9 %all-reduce.3.cloned.1.call-done = f32[128,1024]{1,0:T(8,128)} async-done(((f32[128,1024]{1,0:T(8,128)}), f32[128,1024]{1,0:T(8,128)}) %all-reduce.3.cloned.1.call-update) | async-done | bytes 524304 | tf_op jit(solution)/shard_map/psum | solution.py:26
  97.6 1.8 multiply_reduce_fusion.3
  99.4 13.3 %psum.29 = f32[]{:T(128)} all-reduce(f32[]{:T(128)} %multiply_reduce_fusion.3), channel_id=1, replica_groups=mesh['vec'=4,'row'=8] {'row'}, use_global_device_ids=true, to_apply=%region_2.3 | all-reduce | flops 1 | bytes 8 | tf_op jit(solution)/shard_map/psum | solution.py:27
  113.5 1.9 multiply_divide_fusion.1
  115.4 0.2 all-reduce.5.cloned.1.call-start
  115.6 34.5 %all-gather.3.cloned.1.call-done = f32[1024,1024]{1,0:T(8,128)} async-done(((f32[128,1024]{1,0:T(8,128)}), f32[1024,1024]{1,0:T(8,128)}) %all-gather.3.cloned.1.call-update) | async-done | bytes 4194320 | tf_op jit(solution)/shard_map/all_gather | solution.py:30
  150.1 18.2 %fusion.4 = f32[1024,1024]{1,0:T(8,128)S(1)} fusion(f32[1024,1024]{1,0:T(8,128)} %all-gather.3.cloned.1.call-done), kind=kOutput, calls=%fused_computation.13 | convolution fusion | flops 12890144768 | bytes 8388608 | tf_op jit(solution)/shard_map/dot_general | solution.py:35
  168.3 1.9 copy-done.2
  170.2 109.4 %convolution_bitcast_fusion = f32[32,128,1024]{1,2,0:T(8,128)} fusion(f32[32,128,1024]{2,1,0:T(8,128)} %param.1, f32[1024,1024]{1,0:T(8,128)S(1)} %fusion.4), kind=kOutput, calls=%fused_computation.10 | convolution fusion | flops 51539607552 | bytes 37748736 | tf_op jit(solution)/shard_map/pjk,kl->pjl/dot_general | solution.py:42
  279.7 15.2 %copy.10 = f32[32,128,1024]{1,0,2:T(8,128)S(1)} copy(f32[32,128,1024]{1,2,0:T(8,128)} %convolution_bitcast_fusion) | data formatting | bytes 33554432 | tf_op jit(solution)/shard_map/pjk,kl->pjl/dot_general | solution.py:42
  294.9 186.6 %all_to_all.36 = f32[32,128,1024]{1,0,2:T(8,128)S(1)} all-to-all(f32[32,128,1024]{1,0,2:T(8,128)S(1)} %copy.10), channel_id=1, replica_groups=mesh['vec'=4,'row'=8] {'row'}, dimensions={2} | all-to-all | bytes 33554432 | tf_op jit(solution)/shard_map/all_to_all | solution.py:43
  481.5 19.3 %copy.51 = f32[32,128,8,128]{1,2,3,0:T(8,128)} copy(f32[32,128,8,128]{1,0,3,2:T(8,128)S(1)} %bitcast.66) | data formatting | bytes 33554432 | tf_op jit(solution)/shard_map/all_to_all | solution.py:43
  500.9 18.0 %all_to_all.29 = f32[32,1024,128]{1,2,0:T(8,128)} reshape(f32[32,8,128,128]{2,1,3,0:T(8,128)} %bitcast.67) | data formatting | bytes 33554432 | tf_op jit(solution)/shard_map/all_to_all | solution.py:43
  518.9 57.9 %fusion.10 = f32[32,128,1024]{2,1,0:T(8,128)S(1)} fusion(f32[32,1024,128]{1,2,0:T(8,128)} %all_to_all.29, f32[1024,1024]{1,0:T(8,128)} %copy-done.2), kind=kOutput, calls=%fused_computation.19 | convolution fusion | flops 51539607552 | bytes 37748736 | tf_op jit(solution)/shard_map/pim,ik->pmk/dot_general | solution.py:44
  576.8 6.2 copy-done
  582.9 0.3 constant_dynamic-slice_fusion
  583.2 4.7 copy.12
  587.9 1.8 gather_fusion.1
  589.7 8.9 all_gather.14
  598.6 0.2 copy.39
  598.8 8.3 multiply_reduce_fusion
  607.1 22.2 %fusion = f32[128,1,1024]{2,1,0:T(1,128)S(1)} fusion(f32[32,128,1]{0,2,1:T(1,128)S(1)} %bitcast.72, f32[32,128,1024]{2,1,0:T(8,128)} %copy-done), kind=kOutput, calls=%fused_computation.3 | convolution fusion | flops 50331648 | bytes 17317888 | tf_op jit(solution)/shard_map/pjk,pj->jk/dot_general | solution.py:23
  629.3 0.9 bitcast_subtract_fusion
  630.3 0.0 all-gather.5.cloned.1.call-start
  630.3 38.8 %all-reduce.5.cloned.1.call-done = f32[128,1024]{1,0:T(8,128)} async-done(((f32[128,1024]{1,0:T(8,128)}), f32[128,1024]{1,0:T(8,128)}) %all-reduce.5.cloned.1.call-update) | async-done | bytes 524304 | tf_op jit(solution)/shard_map/psum | solution.py:26
  669.1 1.8 multiply_reduce_fusion.2
  670.9 13.3 %psum.31 = f32[]{:T(128)} all-reduce(f32[]{:T(128)} %multiply_reduce_fusion.2), channel_id=1, replica_groups=mesh['vec'=4,'row'=8] {'row'}, use_global_device_ids=true, to_apply=%region_5.6 | all-reduce | flops 1 | bytes 8 | tf_op jit(solution)/shard_map/psum | solution.py:27
  684.9 1.9 multiply_divide_fusion
  686.8 34.7 %all-gather.5.cloned.1.call-done = f32[1024,1024]{1,0:T(8,128)} async-done(((f32[128,1024]{1,0:T(8,128)}), f32[1024,1024]{1,0:T(8,128)}) %all-gather.5.cloned.1.call-update) | async-done | bytes 4194320 | tf_op jit(solution)/shard_map/all_gather | solution.py:30
  721.6 18.2 %fusion.5 = f32[1024,1024]{1,0:T(8,128)S(1)} fusion(f32[1024,1024]{1,0:T(8,128)} %all-gather.5.cloned.1.call-done), kind=kOutput, calls=%fused_computation.14 | convolution fusion | flops 12890144768 | bytes 8388608 | tf_op jit(solution)/shard_map/dot_general | solution.py:35
  739.8 2.0 copy-done.1
  741.7 58.7 %fusion.8 = f32[32,128,1024]{2,1,0:T(8,128)} fusion(f32[32,128,1024]{2,1,0:T(8,128)} %copy-done, f32[1024,1024]{1,0:T(8,128)S(1)} %fusion.5), kind=kOutput, calls=%fused_computation.17 | convolution fusion | flops 51539607552 | bytes 37748736 | tf_op jit(solution)/shard_map/pjk,kl->pjl/dot_general | solution.py:42
  800.5 17.4 %copy.13 = f32[32,128,1024]{1,0,2:T(8,128)} copy(f32[32,128,1024]{2,1,0:T(8,128)} %fusion.8) | data formatting | bytes 33554432 | tf_op jit(solution)/shard_map/pjk,kl->pjl/dot_general | solution.py:42
  817.8 5.9 all-to-all-start.1
  823.8 5.6 fusion.13
  829.3 178.2 %all-to-all-done.1 = f32[32,128,1024]{1,0,2:T(8,128)} async-done(((f32[32,128,1024]{1,0,2:T(8,128)}), f32[32,128,1024]{1,0,2:T(8,128)}, u32[]{:S(2)}, u32[]{:S(2)}) %all-to-all-start.1) | async-done | bytes 16777248 | tf_op jit(solution)/shard_map/all_to_all | solution.py:43
  1007.5 17.8 %copy.50 = f32[32,128,8,128]{1,2,3,0:T(8,128)} copy(f32[32,128,8,128]{1,0,3,2:T(8,128)} %bitcast.21) | data formatting | bytes 33554432 | tf_op jit(solution)/shard_map/all_to_all | solution.py:43
  1025.3 18.0 %all_to_all.33 = f32[32,1024,128]{1,2,0:T(8,128)} reshape(f32[32,8,128,128]{2,1,3,0:T(8,128)} %bitcast.68) | data formatting | bytes 33554432 | tf_op jit(solution)/shard_map/all_to_all | solution.py:43
  1043.3 61.6 %fusion.6 = f32[32,128,1024]{2,1,0:T(8,128)} fusion(f32[32,1024,128]{1,2,0:T(8,128)} %all_to_all.33, f32[1024,1024]{1,0:T(8,128)} %copy-done.1), kind=kOutput, calls=%fused_computation.15 | convolution fusion | flops 51539607552 | bytes 37748736 | tf_op jit(solution)/shard_map/pim,ik->pmk/dot_general | solution.py:44
  (9 shorter events, 0.1 us)
Async XLA Ops:
  7.2 90.5 %all-reduce.3.cloned.1.call-start = ((), (), s32[]{:S(2)}) async-start(), calls=%async_computation.2 | async-start | bytes 1048576 | tf_op jit(solution)/shard_map/psum | solution.py:26
  58.7 91.4 %all-gather.3.cloned.1.call-start = ((), (), s32[]{:S(2)}) async-start(), calls=%async_computation.3 | async-start | bytes 4718592 | tf_op jit(solution)/shard_map/all_gather | solution.py:30
  115.4 553.7 %all-reduce.5.cloned.1.call-start = ((), (), s32[]{:S(2)}) async-start(), calls=%async_computation.4 | async-start | bytes 1048576 | tf_op jit(solution)/shard_map/psum | solution.py:26
  168.3 1.9 copy-start.2
  576.8 6.2 copy-start
  630.3 91.3 %all-gather.5.cloned.1.call-start = ((), (), s32[]{:S(2)}) async-start(), calls=%async_computation.5 | async-start | bytes 4718592 | tf_op jit(solution)/shard_map/all_gather | solution.py:30
  739.8 2.0 copy-start.1
  817.8 189.7 %all-to-all-start.1 = ((f32[32,128,1024]{1,0,2:T(8,128)}), f32[32,128,1024]{1,0,2:T(8,128)}, u32[]{:S(2)}, u32[]{:S(2)}) async-start(f32[32,128,1024]{1,0,2:T(8,128)} %copy.13), calls=%async_computation.1 | async-start | bytes 33554432 | tf_op jit(solution)/shard_map/all_to_all | solution.py:43
Sparse Core Ops, SparseCore 0:
  58.8 38.7 all-reduce.2
  115.5 34.5 all-gather.2
  630.4 38.6 all-reduce.4
  686.9 34.5 all-gather.4
where the time goes:
time: 1120 us; the launch traced here: 1110 us
  matrix products  374 us (33%)
  waiting for transfers between devices  325 us (29%)
  blocking collectives  234 us (21%)
  local copies, waits for them, and re-layouts  131 us (12%)
  other arithmetic  25.9 us (2%)
  between operations  15.5 us (1%)
    all_to_all x1, blocking collectives, shards(): lax.all_to_all(product_left, 'row', split_axis=2, concat_axis=1, tiled=True)  187 us
    all_to_all x1, waiting for transfers between devices, shards(): lax.all_to_all(product_left, 'row', split_axis=2, concat_axis=1, tiled=True)  178 us
    dot_general x2, matrix products, shards(): jnp.einsum('pjk,kl->pjl', current, step_full, precision=highest)  168 us
    dot_general x2, matrix products, shards(): current = jnp.einsum('pim,ik->pmk', columns, step_full, precision=highest)  120 us
    psum x2, waiting for transfers between devices, shards(): gradient = lax.psum(own_part - other_part, 'vec')  77.7 us
    all_to_all x4, local copies, waits for them, and re-layouts, shards(): lax.all_to_all(product_left, 'row', split_axis=2, concat_axis=1, tiled=True)  73.1 us
    all_gather x2, waiting for transfers between devices, shards(): generator_full = lax.all_gather(generator, 'row', axis=0, tiled=True)  69.3 us
    dot_general x2, matrix products, shards(): own_part = jnp.einsum('pjk,pj->jk', current, diagonal, precision=highest)  44.6 us
  transfers between devices with their start and end apart: 5, of which 5 were waited for; matrix products, arithmetic and copies ran while one was open for 0% of the time, Pallas kernels for 0%

commit v1 on v0

--- a/solution.py
+++ b/solution.py
@@ -40,7 +40,12 @@
         else:
             rotation = jnp.dot(rotation, step_full, precision=highest)
         product_left = jnp.einsum("pjk,kl->pjl", current, step_full, precision=highest)
-        columns = lax.all_to_all(product_left, "row", split_axis=2, concat_axis=1, tiled=True)
+        columns = jnp.concatenate(
+            lax.all_to_all(
+                jnp.stack(jnp.split(product_left, lax.axis_size("row"), axis=2)), "row", 0, 0
+            ),
+            axis=1,
+        )
         current = jnp.einsum("pim,ik->pmk", columns, step_full, precision=highest)
     return (current, rotation)
 

time: 1120 us -> 1060 us (0.946)
  local copies, waits for them, and re-layouts: 131 us -> 60.2 us
  matrix products: 374 us -> 387 us
    all_to_all x4 -> x0, local copies, waits for them, and re-layouts: 73.1 us -> none  [shards(): lax.all_to_all(product_left, 'row', split_axis=2, concat_axis=1, tiled=True)]
    dot_general x2 -> x0, local copies, waits for them, and re-layouts: 32.6 us -> none  [shards(): jnp.einsum('pjk,kl->pjl', current, step_full, precision=highest)]
    reshape x0 -> x2, local copies, waits for them, and re-layouts: none -> 24.6 us  [shards(): jnp.concatenate(lax.all_to_all(jnp.stack(jnp.split(product_left, lax.axis...]
    unnamed x9 -> x25, local copies, waits for them, and re-layouts: 15 us -> 23.5 us
  transfers between devices with their start and end apart: 5 -> 5, of which waited for: 5 -> 5; matrix products, arithmetic and copies ran while one was open for 0% -> 1% of each run, Pallas kernels for 0% -> 0%
where the time goes in v1:
time: 1060 us
  matrix products  387 us (37%)
  waiting for transfers between devices  325 us (31%)
  blocking collectives  235 us (22%)
  local copies, waits for them, and re-layouts  60.2 us (6%)
  other arithmetic  26.2 us (2%)
  between operations  15.8 us (1%)
    all_to_all x1, blocking collectives, shards(): lax.all_to_all(jnp.stack(jnp.split(product_left, lax.axis_size('row'), ax...  188 us
    all_to_all x1, waiting for transfers between devices, shards(): lax.all_to_all(jnp.stack(jnp.split(product_left, lax.axis_size('row'), ax...  178 us
    dot_general x2, matrix products, shards(): jnp.einsum('pjk,kl->pjl', current, step_full, precision=highest)  172 us
    dot_general x2, matrix products, shards(): current = jnp.einsum('pim,ik->pmk', columns, step_full, precision=highest)  129 us
    psum x2, waiting for transfers between devices, shards(): gradient = lax.psum(own_part - other_part, 'vec')  77.7 us
    all_gather x2, waiting for transfers between devices, shards(): generator_full = lax.all_gather(generator, 'row', axis=0, tiled=True)  69.2 us
    dot_general x2, matrix products, shards(): own_part = jnp.einsum('pjk,pj->jk', current, diagonal, precision=highest)  44.6 us
    dot_general x2, matrix products, shards(): jnp.dot(generator_full, generator_full, precision=highest)  36.5 us
  transfers between devices with their start and end apart: 5, of which 5 were waited for; matrix products, arithmetic and copies ran while one was open for 1% of the time, Pallas kernels for 0%

profile of v1, /device:TPU:0, one launch (start us, length us, event | category | flops | bytes accessed | tf_op | source)
XLA Modules:
  0.0 1055.6 jit_solution(4926335506419598859)
XLA Ops:
  7.2 1.7 constant_dynamic-slice_fusion.1
  9.0 4.7 copy.37
  13.6 1.9 gather_fusion
  15.5 11.3 %all_gather.12 = f32[32,1024]{0,1:T(8,128)S(1)} all-gather(f32[32,128]{0,1:T(8,128)S(1)} %bitcast.125), channel_id=1, replica_groups=mesh['vec'=4,'row'=8] {'row'}, dimensions={1}, use_global_device_ids=true | all-gather | bytes 147456 | tf_op jit(solution)/shard_map/all_gather | solution.py:24
  26.8 0.2 copy.38
  27.0 8.5 multiply_reduce_fusion.1
  35.5 22.4 %fusion.2 = f32[128,1,1024]{2,1,0:T(1,128)S(1)} fusion(f32[32,128,1]{0,2,1:T(1,128)S(1)} %bitcast.126, f32[32,128,1024]{2,1,0:T(8,128)} %param.1), kind=kOutput, calls=%fused_computation.6 | convolution fusion | flops 50331648 | bytes 17317888 | tf_op jit(solution)/shard_map/pjk,pj->jk/dot_general | solution.py:23
  57.9 0.9 bitcast_subtract_fusion.1
  58.9 38.9 %all-reduce.3.cloned.1.call-done = f32[128,1024]{1,0:T(8,128)} async-done(((f32[128,1024]{1,0:T(8,128)}), f32[128,1024]{1,0:T(8,128)}) %all-reduce.3.cloned.1.call-update) | async-done | bytes 524304 | tf_op jit(solution)/shard_map/psum | solution.py:26
  97.8 1.8 multiply_reduce_fusion.3
  99.5 13.3 %psum.29 = f32[]{:T(128)} all-reduce(f32[]{:T(128)} %multiply_reduce_fusion.3), channel_id=1, replica_groups=mesh['vec'=4,'row'=8] {'row'}, use_global_device_ids=true, to_apply=%region_2.3 | all-reduce | flops 1 | bytes 8 | tf_op jit(solution)/shard_map/psum | solution.py:27
  113.6 1.9 multiply_divide_fusion.1
  115.5 0.3 all-reduce.5.cloned.1.call-start
  115.8 34.4 %all-gather.3.cloned.1.call-done = f32[1024,1024]{1,0:T(8,128)} async-done(((f32[128,1024]{1,0:T(8,128)}), f32[1024,1024]{1,0:T(8,128)}) %all-gather.3.cloned.1.call-update) | async-done | bytes 4194320 | tf_op jit(solution)/shard_map/all_gather | solution.py:30
  150.2 18.3 %fusion.4 = f32[1024,1024]{1,0:T(8,128)S(1)} fusion(f32[1024,1024]{1,0:T(8,128)} %all-gather.3.cloned.1.call-done), kind=kOutput, calls=%fused_computation.11 | convolution fusion | flops 12890144768 | bytes 8388608 | tf_op jit(solution)/shard_map/dot_general | solution.py:35
  168.5 112.5 %convolution_bitcast_fusion = f32[32,128,1024]{1,2,0:T(8,128)S(1)} fusion(f32[32,128,1024]{2,1,0:T(8,128)} %param.1, f32[1024,1024]{1,0:T(8,128)S(1)} %fusion.4), kind=kOutput, calls=%fused_computation.8 | convolution fusion | flops 51539607552 | bytes 37748736 | tf_op jit(solution)/shard_map/pjk,kl->pjl/dot_general | solution.py:42
  282.2 187.7 %all_to_all.10 = f32[8,32,128,128]{2,3,1,0:T(8,128)} all-to-all(f32[8,32,128,128]{2,3,1,0:T(8,128)S(1)} %fusion.21), channel_id=1, replica_groups=mesh['vec'=4,'row'=8] {'row'}, dimensions={0} | all-to-all | bytes 33554432 | tf_op jit(solution)/shard_map/all_to_all | solution.py:44
  469.9 17.5 %copy.8 = f32[32,8,128,128]{3,2,1,0:T(8,128)} copy(f32[32,8,128,128]{2,3,0,1:T(8,128)} %bitcast.118) | data formatting | bytes 33554432 | tf_op jit(solution)/shard_map/reshape | solution.py:43
  487.4 71.4 %fusion.10 = f32[32,128,1024]{2,1,0:T(8,128)S(1)} fusion(f32[32,1024,128]{2,1,0:T(8,128)} %bitcast.120, f32[1024,1024]{1,0:T(8,128)} %copy-done.3), kind=kOutput, calls=%fused_computation.17 | convolution fusion | flops 51539607552 | bytes 37748736 | tf_op jit(solution)/shard_map/pim,ik->pmk/dot_general | solution.py:49
  558.7 6.2 copy-done
  564.9 0.3 constant_dynamic-slice_fusion
  565.2 4.7 copy.10
  569.9 1.8 gather_fusion.1
  571.7 8.9 all_gather.14
  580.6 0.2 copy.39
  580.7 8.5 multiply_reduce_fusion
  589.2 22.2 %fusion = f32[128,1,1024]{2,1,0:T(1,128)S(1)} fusion(f32[32,128,1]{0,2,1:T(1,128)S(1)} %bitcast.124, f32[32,128,1024]{2,1,0:T(8,128)} %copy-done), kind=kOutput, calls=%fused_computation.3 | convolution fusion | flops 50331648 | bytes 17317888 | tf_op jit(solution)/shard_map/pjk,pj->jk/dot_general | solution.py:23
  611.5 0.9 bitcast_subtract_fusion
  612.5 38.8 %all-reduce.5.cloned.1.call-done = f32[128,1024]{1,0:T(8,128)} async-done(((f32[128,1024]{1,0:T(8,128)}), f32[128,1024]{1,0:T(8,128)}) %all-reduce.5.cloned.1.call-update) | async-done | bytes 524304 | tf_op jit(solution)/shard_map/psum | solution.py:26
  651.2 1.8 multiply_reduce_fusion.2
  653.0 13.3 %psum.31 = f32[]{:T(128)} all-reduce(f32[]{:T(128)} %multiply_reduce_fusion.2), channel_id=1, replica_groups=mesh['vec'=4,'row'=8] {'row'}, use_global_device_ids=true, to_apply=%region_5.6 | all-reduce | flops 1 | bytes 8 | tf_op jit(solution)/shard_map/psum | solution.py:27
  667.0 1.9 multiply_divide_fusion
  669.0 34.7 %all-gather.5.cloned.1.call-done = f32[1024,1024]{1,0:T(8,128)} async-done(((f32[128,1024]{1,0:T(8,128)}), f32[1024,1024]{1,0:T(8,128)}) %all-gather.5.cloned.1.call-update) | async-done | bytes 4194320 | tf_op jit(solution)/shard_map/all_gather | solution.py:30
  703.7 18.3 %fusion.5 = f32[1024,1024]{1,0:T(8,128)S(1)} fusion(f32[1024,1024]{1,0:T(8,128)} %all-gather.5.cloned.1.call-done), kind=kOutput, calls=%fused_computation.12 | convolution fusion | flops 12890144768 | bytes 8388608 | tf_op jit(solution)/shard_map/dot_general | solution.py:35
  722.0 59.2 %fusion.8 = f32[32,128,1024]{2,1,0:T(8,128)S(1)} fusion(f32[32,128,1024]{2,1,0:T(8,128)} %copy-done, f32[1024,1024]{1,0:T(8,128)S(1)} %fusion.5), kind=kOutput, calls=%fused_computation.15 | convolution fusion | flops 51539607552 | bytes 37748736 | tf_op jit(solution)/shard_map/pjk,kl->pjl/dot_general | solution.py:42
  781.2 1.6 fusion.20
  782.8 1.6 fusion.19
  784.5 1.6 fusion.18
  786.1 1.6 fusion.17
  787.7 1.6 fusion.16
  789.3 1.6 fusion.15
  790.9 1.6 fusion.14
  792.6 1.6 fusion.13
  794.2 5.8 all-to-all-start.1
  799.9 5.6 fusion.29
  805.5 178.4 %all-to-all-done.1 = f32[8,32,128,128]{3,2,1,0:T(8,128)} async-done(((f32[8,32,128,128]{3,2,1,0:T(8,128)}), f32[8,32,128,128]{3,2,1,0:T(8,128)}, u32[]{:S(2)}, u32[]{:S(2)}) %all-to-all-start.1) | async-done | bytes 16777248 | tf_op jit(solution)/shard_map/all_to_all | solution.py:44
  983.9 7.1 copy.11
  991.0 57.7 %fusion.6 = f32[32,128,1024]{2,1,0:T(8,128)} fusion(f32[32,1024,128]{2,1,0:T(8,128)S(1)} %bitcast.119, f32[1024,1024]{1,0:T(8,128)S(1)} %copy-done.2), kind=kOutput, calls=%fused_computation.13 | convolution fusion | flops 51539607552 | bytes 37748736 | tf_op jit(solution)/shard_map/pim,ik->pmk/dot_general | solution.py:49
  (23 shorter events, 1.4 us)
Async XLA Ops:
  7.2 90.6 %all-reduce.3.cloned.1.call-start = ((), (), s32[]{:S(2)}) async-start(), calls=%async_computation.2 | async-start | bytes 1048576 | tf_op jit(solution)/shard_map/psum | solution.py:26
  58.8 91.4 %all-gather.3.cloned.1.call-start = ((), (), s32[]{:S(2)}) async-start(), calls=%async_computation.3 | async-start | bytes 4718592 | tf_op jit(solution)/shard_map/all_gather | solution.py:30
  115.5 535.7 %all-reduce.5.cloned.1.call-start = ((), (), s32[]{:S(2)}) async-start(), calls=%async_computation.4 | async-start | bytes 1048576 | tf_op jit(solution)/shard_map/psum | solution.py:26
  168.5 112.5 %copy-start.3 = (f32[1024,1024]{1,0:T(8,128)}, f32[1024,1024]{1,0:T(8,128)S(1)}, u32[]{:S(2)}) copy-start(f32[1024,1024]{1,0:T(8,128)S(1)} %fusion.4) | copy-start | bytes 12582916
  558.7 6.2 copy-start
  612.4 91.3 %all-gather.5.cloned.1.call-start = ((), (), s32[]{:S(2)}) async-start(), calls=%async_computation.5 | async-start | bytes 4718592 | tf_op jit(solution)/shard_map/all_gather | solution.py:30
  722.0 59.2 %copy-start.1 = (f32[1024,1024]{1,0:T(8,128)}, f32[1024,1024]{1,0:T(8,128)S(1)}, u32[]{:S(2)}) copy-start(f32[1024,1024]{1,0:T(8,128)S(1)} %fusion.5) | copy-start | bytes 12582916
  794.2 189.7 %all-to-all-start.1 = ((f32[8,32,128,128]{3,2,1,0:T(8,128)}), f32[8,32,128,128]{3,2,1,0:T(8,128)}, u32[]{:S(2)}, u32[]{:S(2)}) async-start(f32[8,32,128,128]{3,2,1,0:T(8,128)} %fusion.13), calls=%async_computation.1 | async-start | bytes 33554432 | tf_op jit(solution)/shard_map/all_to_all | solution.py:44
  983.9 7.1 copy-start.2
Sparse Core Ops, SparseCore 0:
  58.9 38.7 all-reduce.2
  115.6 34.5 all-gather.2
  612.5 38.6 all-reduce.4
  669.1 34.5 all-gather.4
